TPU v7x, 128 devices: a whole 4x4x4 slice. The times are simulated.
128 devices in a mesh: shard: 16 (over z, x), context: 4 (over y), tensor: 2 (over core).
Axes of the slice: x: 4, y: 4, z: 4, core: 2. Of those that a mesh axis runs over, the one named last changes fastest.
Arguments:
- inputs: float32 [32, 512, 768], P('shard', 'context'), may hold values from -6 to 6
- segment_ids: int32 [32, 512], P('shard', 'context'), may hold values from 0 to 3, never falling along the last dimension, each value on 1 to 256 neighbouring positions
- projection: bfloat16 [2, 3, 768, 768], P(None, None, 'shard', 'tensor'), may hold values from -1 to 1
- head_bias: bfloat16 [2, 2, 12, 64], P(None, None, 'tensor', 'shard'), may hold values from -3 to 3
- mixing: bfloat16 [2, 768, 768], P(None, 'tensor', 'shard'), may hold values from -0.875 to 0.875
- expansion: bfloat16 [2, 768, 3072], P(None, 'shard', 'tensor'), may hold values from -0.21875 to 0.21875
- hidden_bias: bfloat16 [2, 48, 64], P(None, 'tensor', 'shard'), may hold values from -3 to 3
- contraction: bfloat16 [2, 3072, 768], P(None, 'tensor', 'shard'), may hold values from -0.109375 to 0.109375
- norm_gains: bfloat16 [2, 2, 768], P(None, None, 'shard'), may hold values from 0.3984375 to 1.59375
- offsets: bfloat16 [2, 4, 768], P(None, None, 'shard'), may hold values from -2 to 2
- cotangent: float32 [32, 512, 768], P('shard', 'context'), may hold values from -6 to 6
Outputs:
- outputs: float32 [32, 512, 768], P('shard', 'context')
- input_grad: float32 [32, 512, 768], P('shard', 'context')
- grad_projection: float32 [2, 3, 768, 768], P(None, None, 'shard', 'tensor')
- head_grad: float32 [2, 2, 12, 64], P(None, None, 'tensor', 'shard')
- grad_mixing: float32 [2, 768, 768], P(None, 'tensor', 'shard')
- grad_expansion: float32 [2, 768, 3072], P(None, 'shard', 'tensor')
- hidden_grad: float32 [2, 48, 64], P(None, 'tensor', 'shard')
- grad_contraction: float32 [2, 3072, 768], P(None, 'tensor', 'shard')
- gains_grad: float32 [2, 2, 768], P(None, None, 'shard')
- grad_offsets: float32 [2, 4, 768], P(None, None, 'shard')
Inputs may be any that keep to these rules, and one draw needn't show every extreme that they name: `segment_ids`: within a row ids never fall; every document holds 1 to 256 positions and in every row some document holds exactly 256.
All inputs are finite; a program needn't handle non-finite values.
Results may differ from a plain program's by a relative error of at most 0.033.
Values may be sent and summed in bfloat16 or wider, within the bound.
No kernel may reach another device: no remote copies, remote signals or barrier semaphores. Data moves between devices by JAX's collectives and lax.ppermute only.
A program may use at most 128 MiB of HBM per device.

v0:
```python
import jax
import jax.numpy as jnp
from jax import lax
from jax.sharding import PartitionSpec as P

HEAD = 64
EPS = 1e-05
GELU_COEF = 0.7978845608028654
GELU_CUBE = 0.044715
MASKED = -1e30
HALF = jnp.bfloat16
FULL = jnp.float32


def gelu_value(preact):
    inner_arg = GELU_COEF * (preact + GELU_CUBE * preact * preact * preact)
    return 0.5 * preact * (1.0 + jnp.tanh(inner_arg))


def gelu_slope(preact):
    inner_arg = GELU_COEF * (preact + GELU_CUBE * preact * preact * preact)
    tanh_value = jnp.tanh(inner_arg)
    return 0.5 * (1.0 + tanh_value) + 0.5 * preact * (1.0 - tanh_value * tanh_value) * GELU_COEF * (
        1.0 + 3.0 * GELU_CUBE * preact * preact
    )


def norm_forward(stream):
    center = stream - jnp.mean(stream, axis=-1, keepdims=True)
    spread = lax.rsqrt(jnp.mean(center * center, axis=-1, keepdims=True) + EPS)
    return (center * spread, spread)


def norm_backward(upstream, normed, spread, gain_row):
    scaled = upstream * gain_row
    first_mean = jnp.mean(scaled, axis=-1, keepdims=True)
    second_mean = jnp.mean(scaled * normed, axis=-1, keepdims=True)
    return spread * (scaled - first_mean - normed * second_mean)


def dot(left, right, left_dim, right_dim):
    return lax.dot_general(
        left, right, (((left_dim,), (right_dim,)), ((), ())), preferred_element_type=FULL
    )


def pair_sum(part):
    size = lax.axis_size("tensor")
    other = lax.ppermute(part, "tensor", [(i, (i + 1) % size) for i in range(size)])
    return part.astype(FULL) + other.astype(FULL)


def from_before(block, steps):
    size = lax.axis_size("context")
    return lax.ppermute(block, "context", [(i, i + steps) for i in range(size - steps)])


def from_after(block, steps):
    size = lax.axis_size("context")
    return lax.ppermute(block, "context", [(i + steps, i) for i in range(size - steps)])


def context_sum(part):
    size = lax.axis_size("context")
    total = part.astype(FULL)
    for steps in range(1, size):
        moved = lax.ppermute(part, "context", [(i, (i + steps) % size) for i in range(size)])
        total = total + moved.astype(FULL)
    return total


def masked_scores(query_block, key_block, visible, head_scale):
    scores = (
        jnp.einsum("rqhe,rkhe->rhqk", query_block, key_block, preferred_element_type=FULL)
        * head_scale
    )
    return jnp.where(visible, scores, MASKED)


def per_device(
    inputs,
    segment_ids,
    projection,
    head_bias,
    mixing,
    expansion,
    hidden_bias,
    contraction,
    norm_gains,
    offsets,
    cotangent,
):
    layers = projection.shape[0]
    rows, block, width = inputs.shape
    shards = lax.axis_size("shard")
    contexts = lax.axis_size("context")
    own = projection.shape[2]
    heads = head_bias.shape[2]
    head_cols = projection.shape[3]
    hidden = expansion.shape[2]
    tokens = rows * block
    head_scale = HEAD ** (-0.5)
    back_steps = 2
    gathered = []
    for layer in range(layers):
        packed = jnp.concatenate(
            [
                projection[layer, 0],
                projection[layer, 1],
                projection[layer, 2],
                mixing[layer].T,
                expansion[layer],
                contraction[layer].T,
            ],
            axis=1,
        )
        gathered.append(lax.all_gather(packed, "shard", axis=0, tiled=True))
    small_parts = [norm_gains, offsets, head_bias, hidden_bias]
    small_sizes = [part.size for part in small_parts]
    small_total = sum(small_sizes)
    small_padded = -(-small_total // 1024) * 1024
    small = jnp.concatenate(
        [part.reshape(-1) for part in small_parts]
        + [jnp.zeros((small_padded - small_total,), HALF)]
    )
    small = jnp.broadcast_to(small.reshape(1, -1, 128), (shards, small_padded // 128, 128))
    small = lax.all_to_all(small, "shard", 0, 0).reshape(shards, small_padded)

    def widen(index):
        start = sum(small_sizes[:index])
        shape = small_parts[index].shape
        piece = small[:, start : start + small_sizes[index]].astype(FULL).reshape((shards,) + shape)
        piece = jnp.moveaxis(piece, 0, -2)
        return piece.reshape(shape[:-1] + (shards * shape[-1],))

    gains_all, offsets_all = (widen(0), widen(1))
    head_all = widen(2).reshape(layers, 2, head_cols)
    hidden_all = widen(3).reshape(layers, hidden)
    seg_before = [from_before(segment_ids, steps) for steps in range(back_steps, 0, -1)]
    segments_all = jnp.concatenate(seg_before + [segment_ids], axis=1)
    query_pos = jnp.arange(block, dtype=jnp.int32) + back_steps * block
    key_pos = jnp.arange((back_steps + 1) * block, dtype=jnp.int32)
    first_key = (back_steps - lax.axis_index("context")) * block
    visible = (
        (segments_all[:, None, :] == segment_ids[:, :, None])
        & (key_pos[None, None, :] <= query_pos[None, :, None])
        & (key_pos >= first_key)[None, None, :]
    )
    visible = visible[:, None]

    def split_weights(weights):
        ends = [3 * head_cols, 4 * head_cols, 4 * head_cols + hidden, 4 * head_cols + 2 * hidden]
        return (
            weights[:, : ends[0]],
            weights[:, ends[0] : ends[1]],
            weights[:, ends[1] : ends[2]],
            weights[:, ends[2] : ends[3]],
        )

    stream = inputs.reshape(tokens, width)
    kept = []
    for layer in range(layers):
        qkv_weight, out_weight, up_weight, down_weight = split_weights(gathered[layer])
        gain, offset = (gains_all[layer], offsets_all[layer])
        normed_one, spread_one = norm_forward(stream)
        attend_input = (normed_one * gain[0] + offset[0]).astype(HALF)
        zero_bias = jnp.zeros((head_cols,), FULL)
        bias = jnp.concatenate([head_all[layer, 0], zero_bias, head_all[layer, 1]])
        projected = (dot(attend_input, qkv_weight, 1, 0) + bias).astype(HALF)
        query_rows = projected[:, :head_cols]
        key_value = projected[:, head_cols:].reshape(rows, block, 2 * head_cols)
        before = [from_before(key_value, steps) for steps in range(back_steps, 0, -1)]
        key_value_all = jnp.concatenate(before + [key_value], axis=1)
        query_block = query_rows.reshape(rows, block, heads, HEAD)
        key_block = key_value_all[:, :, :head_cols].reshape(rows, -1, heads, HEAD)
        value_block = key_value_all[:, :, head_cols:].reshape(rows, -1, heads, HEAD)
        masked = masked_scores(query_block, key_block, visible, head_scale)
        row_top = jnp.max(masked, axis=-1, keepdims=True)
        log_total = row_top + jnp.log(jnp.sum(jnp.exp(masked - row_top), axis=-1, keepdims=True))
        soft_half = jnp.exp(masked - log_total).astype(HALF)
        attended = (
            jnp.einsum("rhqk,rkhe->rqhe", soft_half, value_block, preferred_element_type=FULL)
            .astype(HALF)
            .reshape(tokens, head_cols)
        )
        middle = stream + pair_sum(dot(attended, out_weight, 1, 1)) + offset[2]
        normed_two, spread_two = norm_forward(middle)
        feed_input = (normed_two * gain[1] + offset[1]).astype(HALF)
        preact = dot(feed_input, up_weight, 1, 0) + hidden_all[layer]
        activation = gelu_value(preact).astype(HALF)
        stream = middle + pair_sum(dot(activation, down_weight, 1, 1)) + offset[3]
        kept.append(
            (
                normed_one,
                spread_one,
                attend_input,
                query_block,
                key_block,
                value_block,
                log_total,
                attended,
                normed_two,
                spread_two,
                feed_input,
                preact,
                activation,
            )
        )

    def scatter(parts):
        packed = jnp.concatenate([part.astype(HALF) for part in parts], axis=1)
        return lax.psum_scatter(packed, "shard", scatter_dimension=0, tiled=True)

    upstream = cotangent.reshape(tokens, width)
    feed_shares, attend_shares, vectors = ([None] * layers, [None] * layers, [None] * layers)
    for layer in reversed(range(layers)):
        (
            normed_one,
            spread_one,
            attend_input,
            query_block,
            key_block,
            value_block,
            log_total,
            attended,
            normed_two,
            spread_two,
            feed_input,
            preact,
            activation,
        ) = kept[layer]
        qkv_weight, out_weight, up_weight, down_weight = split_weights(gathered[layer])
        gain = gains_all[layer]
        upstream_half = upstream.astype(HALF)
        contraction_part = dot(upstream_half, activation, 0, 0)
        offset_down = jnp.sum(upstream, axis=0)
        hidden_back = dot(upstream_half, down_weight, 1, 0) * gelu_slope(preact)
        hidden_half = hidden_back.astype(HALF)
        hidden_part = jnp.sum(hidden_back, axis=0)
        expansion_part = dot(feed_input, hidden_half, 0, 0)
        feed_shares[layer] = scatter([expansion_part, contraction_part])
        feed_back = pair_sum(dot(hidden_half, up_weight, 1, 1).astype(HALF))
        gain_two = jnp.sum(feed_back * normed_two, axis=0)
        offset_two = jnp.sum(feed_back, axis=0)
        middle_back = upstream + norm_backward(feed_back, normed_two, spread_two, gain[1])
        middle_half = middle_back.astype(HALF)
        mixing_part = dot(middle_half, attended, 0, 0)
        offset_mix = jnp.sum(middle_back, axis=0)
        attended_back = dot(middle_half, out_weight, 1, 0).astype(HALF)
        back_heads = attended_back.reshape(rows, block, heads, HEAD)
        attended_heads = attended.reshape(rows, block, heads, HEAD)
        row_delta = jnp.sum(back_heads.astype(FULL) * attended_heads.astype(FULL), axis=-1)
        masked = masked_scores(query_block, key_block, visible, head_scale)
        soft = jnp.exp(masked - log_total)
        soft_half = soft.astype(HALF)
        prob_back = jnp.einsum(
            "rqhe,rkhe->rhqk", back_heads, value_block, preferred_element_type=FULL
        )
        score_back = (
            soft * (prob_back - jnp.transpose(row_delta, (0, 2, 1))[..., None]) * head_scale
        ).astype(HALF)
        query_back = jnp.einsum(
            "rhqk,rkhe->rqhe", score_back, key_block, preferred_element_type=FULL
        ).reshape(tokens, head_cols)
        key_full = jnp.einsum(
            "rhqk,rqhe->rkhe", score_back, query_block, preferred_element_type=FULL
        ).reshape(rows, -1, head_cols)
        value_full = jnp.einsum(
            "rhqk,rqhe->rkhe", soft_half, back_heads, preferred_element_type=FULL
        ).reshape(rows, -1, head_cols)
        both_full = jnp.concatenate([key_full, value_full], axis=2)
        both_back = both_full[:, back_steps * block :]
        for steps in range(1, back_steps + 1):
            start = (back_steps - steps) * block
            both_back = both_back + from_after(
                both_full[:, start : start + block].astype(HALF), steps
            ).astype(FULL)
        both_back = both_back.reshape(tokens, 2 * head_cols)
        head_part = jnp.concatenate(
            [jnp.sum(query_back, axis=0), jnp.sum(both_back[:, head_cols:], axis=0)]
        )
        project_back = jnp.concatenate([query_back, both_back], axis=1).astype(HALF)
        projection_part = dot(attend_input, project_back, 0, 0)
        attend_shares[layer] = scatter([projection_part, mixing_part])
        input_back = pair_sum(dot(project_back, qkv_weight, 1, 1).astype(HALF))
        gain_one = jnp.sum(input_back * normed_one, axis=0)
        offset_one = jnp.sum(input_back, axis=0)
        upstream = middle_back + norm_backward(input_back, normed_one, spread_one, gain[0])
        vectors[layer] = (
            [gain_one, gain_two],
            [offset_one, offset_two, offset_mix, offset_down],
            head_part,
            hidden_part,
        )

    def spread_out(values, shape):
        lead = shape[:-1]
        values = values.reshape(lead + (shards, shape[-1]))
        return jnp.moveaxis(values, -2, 0).reshape(shards, -1)

    gain_sums = jnp.stack([jnp.stack(entry[0]) for entry in vectors])
    offset_sums = jnp.stack([jnp.stack(entry[1]) for entry in vectors])
    head_sums = jnp.stack([entry[2] for entry in vectors])
    hidden_sums = jnp.stack([entry[3] for entry in vectors])
    vector_pack = jnp.concatenate(
        [
            spread_out(values, part.shape)
            for values, part in zip((gain_sums, offset_sums, head_sums, hidden_sums), small_parts)
        ]
        + [jnp.zeros((shards, small_padded - small_total), FULL)],
        axis=1,
    )
    vector_pack = lax.all_to_all(vector_pack.reshape(shards, -1, 128), "shard", 0, 0)
    vector_own = context_sum(jnp.sum(vector_pack, axis=0)).reshape(-1)
    vector_out = []
    for index, part in enumerate(small_parts):
        start = sum(small_sizes[:index])
        vector_out.append(vector_own[start : start + small_sizes[index]].reshape(part.shape))
    gains_grad, offsets_grad, head_grad, hidden_grad = vector_out
    feed_own = [context_sum(share) for share in feed_shares]
    attend_own = [context_sum(share) for share in attend_shares]
    projection_grad = jnp.stack(
        [
            jnp.stack([share[:, k * head_cols : (k + 1) * head_cols] for k in range(3)])
            for share in attend_own
        ]
    )
    mixing_grad = jnp.stack([share[:, 3 * head_cols :].T for share in attend_own])
    expansion_grad = jnp.stack([share[:, :hidden] for share in feed_own])
    contraction_grad = jnp.stack([share[:, hidden:].T for share in feed_own])
    return (
        stream.reshape(rows, block, width),
        upstream.reshape(rows, block, width),
        projection_grad,
        head_grad,
        mixing_grad,
        expansion_grad,
        hidden_grad,
        contraction_grad,
        gains_grad,
        offsets_grad,
    )


def solution(mesh):
    in_specs = (
        P("shard", "context", None),
        P("shard", "context"),
        P(None, None, "shard", "tensor"),
        P(None, None, "tensor", "shard"),
        P(None, "tensor", "shard"),
        P(None, "shard", "tensor"),
        P(None, "tensor", "shard"),
        P(None, "tensor", "shard"),
        P(None, None, "shard"),
        P(None, None, "shard"),
        P("shard", "context", None),
    )
    out_specs = (
        P("shard", "context", None),
        P("shard", "context", None),
        P(None, None, "shard", "tensor"),
        P(None, None, "tensor", "shard"),
        P(None, "tensor", "shard"),
        P(None, "shard", "tensor"),
        P(None, "tensor", "shard"),
        P(None, "tensor", "shard"),
        P(None, None, "shard"),
        P(None, None, "shard"),
    )
    return jax.shard_map(
        per_device, mesh=mesh, in_specs=in_specs, out_specs=out_specs, check_vma=False
    )
```

profile of v0, /device:TPU:0, one launch (start us, length us, event | category | flops | bytes accessed | tf_op | source)
XLA Modules:
  0.0 616.7 jit_solution(8124101954752828164)
XLA Ops:
  14.1 5.2 collective-permute-start.2
  19.3 2.6 collective-permute-start.3
  23.3 7.9 %all-to-all-start = ((bf16[16,8,128]{2,1,0:T(8,128)(2,1)}), bf16[16,8,128]{2,1,0:T(8,128)(2,1)S(1)}, u32[]{:S(2)}, u32[]{:S(2)}) async-start(bf16[16,8,128]{2,1,0:T(8,128)(2,1)} %broadcast_in_dim.34), calls=%async_computation | async-start | bytes 65536 | tf_op jit(solution)/shard_map/all_to_all | solution.py:127
  31.7 7.1 %all-to-all-done = bf16[16,8,128]{2,1,0:T(8,128)(2,1)S(1)} async-done(((bf16[16,8,128]{2,1,0:T(8,128)(2,1)}), bf16[16,8,128]{2,1,0:T(8,128)(2,1)S(1)}, u32[]{:S(2)}, u32[]{:S(2)}) %all-to-all-start) | async-done | bytes 32800 | tf_op jit(solution)/shard_map/all_to_all | solution.py:127
  42.3 39.0 %all-gather.3.cloned.1.call-done = bf16[768,4608]{1,0:T(8,128)(2,1)} async-done(((bf16[48,4608]{1,0:T(8,128)(2,1)}), bf16[768,4608]{1,0:T(8,128)(2,1)}) %all-gather.3.cloned.1.call-update) | async-done | bytes 7077904 | tf_op jit(solution)/shard_map/all_gather | solution.py:117
  81.2 2.2 fusion.2
  83.5 4.9 collective-permute-start
  88.4 2.5 collective-permute-start.1
  91.4 6.5 %collective-permute-done = bf16[2,128,768]{2,1,0:T(8,128)(2,1)S(1)} collective-permute-done((bf16[2,128,768]{2,1,0:T(8,128)(2,1)S(1)}, bf16[2,128,768]{2,1,0:T(8,128)(2,1)S(1)}, u32[]{:S(2)}, u32[]{:S(2)}) %collective-permute-start) | collective-permute-done | bytes 393248 | tf_op jit(solution)/shard_map/ppermute | solution.py:55
  97.9 7.3 %collective-permute-done.1 = bf16[2,128,768]{2,1,0:T(8,128)(2,1)S(1)} collective-permute-done((bf16[2,128,768]{2,1,0:T(8,128)(2,1)S(1)}, bf16[2,128,768]{2,1,0:T(8,128)(2,1)S(1)}, u32[]{:S(2)}, u32[]{:S(2)}) %collective-permute-start.1) | collective-permute-done | bytes 393248 | tf_op jit(solution)/shard_map/ppermute | solution.py:55
  112.0 2.4 fusion.74
  126.0 2.6 convolution_add_fusion.3
  128.6 4.2 fusion.15
  133.6 2.0 collective-permute-done.5
  138.5 10.1 %all-gather.5.cloned.1.call-done = bf16[768,4608]{1,0:T(8,128)(2,1)} async-done(((bf16[48,4608]{1,0:T(8,128)(2,1)}), bf16[768,4608]{1,0:T(8,128)(2,1)}) %all-gather.5.cloned.1.call-update) | async-done | bytes 7077904 | tf_op jit(solution)/shard_map/all_gather | solution.py:117
  148.6 2.5 fusion.3
  151.9 5.7 collective-permute-start.6
  157.6 3.4 collective-permute-start.7
  162.8 3.9 collective-permute-done.6
  166.7 7.3 %collective-permute-done.7 = bf16[2,128,768]{2,1,0:T(8,128)(2,1)} collective-permute-done((bf16[2,128,768]{2,1,0:T(8,128)(2,1)}, bf16[2,128,768]{2,1,0:T(8,128)(2,1)}, u32[]{:S(2)}, u32[]{:S(2)}) %collective-permute-start.7) | collective-permute-done | bytes 393248 | tf_op jit(solution)/shard_map/ppermute | solution.py:55
  176.4 2.1 copy.175
  182.4 2.1 copy.173
  184.6 2.6 fusion.49
  187.4 2.5 fusion.71
  200.9 2.7 convolution_add_fusion.2
  203.6 4.2 fusion.135
  210.0 1.9 fusion.9
  212.3 2.5 multiply_reduce_fusion
  214.8 3.5 fusion.119
  223.5 3.5 fusion.80
  227.0 1.9 multiply_convert_fusion.1
  228.9 2.7 copy.186
  231.6 2.6 fusion.100
  234.2 2.7 copy.185
  246.2 7.9 %collective-permute-done.11 = bf16[2,128,768]{2,1,0:T(8,128)(2,1)} collective-permute-done((bf16[2,128,768]{2,1,0:T(8,128)(2,1)}, bf16[2,128,768]{2,1,0:T(8,128)(2,1)}, u32[]{:S(2)}, u32[]{:S(2)}) %collective-permute-start.11) | collective-permute-done | bytes 393248 | tf_op jit(solution)/shard_map/ppermute | solution.py:60
  254.1 3.1 collective-permute-done.12
  259.8 2.3 fusion.39
  266.5 2.0 fusion.136
  272.3 2.5 multiply_reduce_fusion.2
  274.9 2.1 fusion.117
  282.7 2.7 copy.195
  286.4 1.9 multiply_convert_fusion
  298.5 15.0 %collective-permute-done.15 = bf16[2,128,768]{2,1,0:T(8,128)(2,1)} collective-permute-done((bf16[2,128,768]{2,1,0:T(8,128)(2,1)}, bf16[2,128,768]{2,1,0:T(8,128)(2,1)}, u32[]{:S(2)}, u32[]{:S(2)}) %collective-permute-start.15) | collective-permute-done | bytes 393248 | tf_op jit(solution)/shard_map/ppermute | solution.py:60
  313.5 3.2 collective-permute-done.16
  325.4 2.7 pad_maximum_fusion.1
  329.3 2.2 convolution_convert_fusion.3
  332.5 2.7 pad_maximum_fusion
  341.0 2.3 fusion.36
  352.5 5.3 all-to-all-start.1
  357.8 7.6 %all-to-all-done.1 = f32[16,8,128]{2,1,0:T(8,128)S(1)} async-done(((f32[16,8,128]{2,1,0:T(8,128)}), f32[16,8,128]{2,1,0:T(8,128)S(1)}, u32[]{:S(2)}, u32[]{:S(2)}) %all-to-all-start.1) | async-done | bytes 65568 | tf_op jit(solution)/shard_map/all_to_all | solution.py:313
  365.5 7.0 %collective-permute-start.24 = (f32[8,128]{1,0:T(8,128)S(1)}, f32[8,128]{1,0:T(8,128)S(1)}, u32[]{:S(2)}, u32[]{:S(2)}) collective-permute-start(f32[8,128]{1,0:T(8,128)S(1)} %reduce_sum.395), channel_id=1, source_target_pairs={{0,2},{2,4},{4,6},{6,0},{1,3},{3,5},{5,7},{7,1},{8,10},{10,12},{12... | collective-permute-start | bytes 12296 | tf_op jit(solution)/shard_map/ppermute | solution.py:67
  372.5 2.8 collective-permute-start.26
  377.8 3.8 collective-permute-start.22
  388.0 41.1 %reduce-scatter.5.cloned.1.call-done = bf16[48,1536]{1,0:T(8,128)(2,1)} async-done(((bf16[768,1536]{1,0:T(8,128)(2,1)}), bf16[48,1536]{1,0:T(8,128)(2,1)}) %reduce-scatter.5.cloned.1.call-update) | async-done | bytes 147472 | tf_op jit(solution)/shard_map/reduce_scatter | solution.py:212
  430.6 2.7 collective-permute-start.19
  434.8 2.2 collective-permute-done.18
  439.6 70.3 %reduce-scatter.11.cloned.1.call-done = bf16[48,3072]{1,0:T(8,128)(2,1)} async-done(((bf16[768,3072]{1,0:T(8,128)(2,1)}), bf16[48,3072]{1,0:T(8,128)(2,1)}) %reduce-scatter.11.cloned.1.call-update) | async-done | bytes 294928 | tf_op jit(solution)/shard_map/reduce_scatter | solution.py:212
  511.4 2.7 collective-permute-start.31
  517.1 3.2 collective-permute-done.30
  520.3 5.5 collective-permute-done.31
  526.0 64.9 %reduce-scatter.9.cloned.1.call-done = bf16[48,3072]{1,0:T(8,128)(2,1)} async-done(((bf16[768,3072]{1,0:T(8,128)(2,1)}), bf16[48,3072]{1,0:T(8,128)(2,1)}) %reduce-scatter.9.cloned.1.call-update) | async-done | bytes 294928 | tf_op jit(solution)/shard_map/reduce_scatter | solution.py:212
  592.3 2.7 collective-permute-start.28
  596.5 4.8 collective-permute-done.27
  601.3 5.5 collective-permute-done.28
  (498 shorter events, 149.2 us)
Async XLA Ops:
  7.2 14.7 %copy-start.107 = (bf16[2,24,4]{1,2,0:T(4,128)(2,1)S(1)}, bf16[2,24,4]{1,2,0:T(4,128)(2,1)}, u32[]{:S(2)}) copy-start(bf16[2,24,4]{1,2,0:T(4,128)(2,1)} %param.17) | copy-start | bytes 1156
  7.2 15.0 %copy-start.106 = (bf16[2,2,6,4]{2,3,1,0:T(4,128)(2,1)S(1)}, bf16[2,2,6,4]{2,3,1,0:T(4,128)(2,1)}, u32[]{:S(2)}) copy-start(bf16[2,2,6,4]{2,3,1,0:T(4,128)(2,1)} %param.14) | copy-start | bytes 580
  7.2 15.2 %copy-start.108 = (bf16[2,4,48]{2,1,0:T(4,128)(2,1)S(1)}, bf16[2,4,48]{2,1,0:T(4,128)(2,1)}, u32[]{:S(2)}) copy-start(bf16[2,4,48]{2,1,0:T(4,128)(2,1)} %param.20) | copy-start | bytes 2308
  7.2 15.3 %copy-start.109 = (bf16[2,2,48]{2,1,0:T(2,128)(2,1)S(1)}, bf16[2,2,48]{2,1,0:T(2,128)(2,1)}, u32[]{:S(2)}) copy-start(bf16[2,2,48]{2,1,0:T(2,128)(2,1)} %param.19) | copy-start | bytes 1156
  7.2 24.0 %copy-start.2 = (f32[2,128,768]{2,1,0:T(8,128)S(1)}, f32[2,128,768]{2,1,0:T(8,128)}, u32[]{:S(2)}) copy-start(f32[2,128,768]{2,1,0:T(8,128)} %param.11) | copy-start | bytes 2359300
  7.2 74.0 %all-gather.3.cloned.1.call-start = ((), (), s32[]{:S(2)}) async-start(), calls=%async_computation.6 | async-start | bytes 7520256 | tf_op jit(solution)/shard_map/all_gather | solution.py:117
  13.4 135.2 %all-gather.5.cloned.1.call-start = ((), (), s32[]{:S(2)}) async-start(), calls=%async_computation.7 | async-start | bytes 7520256 | tf_op jit(solution)/shard_map/all_gather | solution.py:117
  14.1 76.8 %collective-permute-start.2 = (s32[2,128]{1,0:T(2,128)S(1)}, s32[2,128]{1,0:T(2,128)S(1)}, u32[]{:S(2)}, u32[]{:S(2)}) collective-permute-start(s32[2,128]{1,0:T(2,128)S(1)} %copy-done.105), channel_id=1, source_target_pairs={{0,4},{2,6},{1,5},{3,7},{8,12},{10,14},{9,13},{11,15},{16,20},{18,... | collective-permute-start | bytes 3080 | tf_op jit(solution)/shard_map/ppermute | solution.py:55
  19.3 71.7 %collective-permute-start.3 = (s32[2,128]{1,0:T(2,128)S(1)}, s32[2,128]{1,0:T(2,128)S(1)}, u32[]{:S(2)}, u32[]{:S(2)}) collective-permute-start(s32[2,128]{1,0:T(2,128)S(1)} %copy-done.105), channel_id=1, source_target_pairs={{0,2},{2,4},{4,6},{1,3},{3,5},{5,7},{8,10},{10,12},{12,14},{9,11},... | collective-permute-start | bytes 3080 | tf_op jit(solution)/shard_map/ppermute | solution.py:55
  23.3 15.6 %all-to-all-start = ((bf16[16,8,128]{2,1,0:T(8,128)(2,1)}), bf16[16,8,128]{2,1,0:T(8,128)(2,1)S(1)}, u32[]{:S(2)}, u32[]{:S(2)}) async-start(bf16[16,8,128]{2,1,0:T(8,128)(2,1)} %broadcast_in_dim.34), calls=%async_computation | async-start | bytes 65536 | tf_op jit(solution)/shard_map/all_to_all | solution.py:127
  31.2 346.6 %reduce-scatter.7.cloned.1.call-start = ((), (), s32[]{:S(2)}) async-start(), calls=%async_computation.9 | async-start | bytes 2506752 | tf_op jit(solution)/shard_map/reduce_scatter | solution.py:212
  31.4 52.0 %copy-start.80 = (f32[256]{0:T(256)}, f32[256]{0:T(256)S(1)}, u32[]{:S(2)}) copy-start(f32[256]{0:T(256)S(1)} %get-tuple-element.151) | copy-start | bytes 3076
  31.7 51.7 %copy-start.82 = (f32[256]{0:T(256)}, f32[256]{0:T(256)S(1)}, u32[]{:S(2)}) copy-start(f32[256]{0:T(256)S(1)} %rsqrt_bitcast_fusion) | copy-start | bytes 3076
  40.8 42.6 %copy-start.58 = (f32[768]{0:T(1024)}, f32[768]{0:T(1024)S(1)}, u32[]{:S(2)}) copy-start(f32[768]{0:T(1024)S(1)} %mul.315) | copy-start | bytes 9220
  42.3 39.0 %copy-start.42 = (bf16[256,768]{1,0:T(8,128)(2,1)}, bf16[256,768]{1,0:T(8,128)(2,1)S(1)}, u32[]{:S(2)}) copy-start(bf16[256,768]{1,0:T(8,128)(2,1)S(1)} %add_convert_fusion.3) | copy-start | bytes 1179652
  83.5 14.5 %collective-permute-start = (bf16[2,128,768]{2,1,0:T(8,128)(2,1)S(1)}, bf16[2,128,768]{2,1,0:T(8,128)(2,1)S(1)}, u32[]{:S(2)}, u32[]{:S(2)}) collective-permute-start(bf16[2,128,768]{2,1,0:T(8,128)(2,1)S(1)} %bitcast.247), channel_id=1, source_target_pairs={{0,4},{2,6},{1,5},{3,7},{8,12},{10,14},{9,13},{11,15},{16,20},{18,... | collective-permute-start | bytes 1179656 | tf_op jit(solution)/shard_map/ppermute | solution.py:55
  88.4 16.8 %collective-permute-start.1 = (bf16[2,128,768]{2,1,0:T(8,128)(2,1)S(1)}, bf16[2,128,768]{2,1,0:T(8,128)(2,1)S(1)}, u32[]{:S(2)}, u32[]{:S(2)}) collective-permute-start(bf16[2,128,768]{2,1,0:T(8,128)(2,1)S(1)} %bitcast.248), channel_id=1, source_target_pairs={{0,2},{2,4},{4,6},{1,3},{3,5},{5,7},{8,10},{10,12},{12,14},{9,11},... | collective-permute-start | bytes 1179656 | tf_op jit(solution)/shard_map/ppermute | solution.py:55
  91.2 16.4 %copy-start.44 = (pred[2,128,384]{2,1,0:T(8,128)(4,1)}, pred[2,128,384]{2,1,0:T(8,128)(4,1)S(1)}, u32[]{:S(2)}) copy-start(pred[2,128,384]{2,1,0:T(8,128)(4,1)S(1)} %and_and_fusion) | copy-start | bytes 294916
  114.4 8.5 %collective-permute-start.4 = (f32[256,768]{1,0:T(8,128)}, f32[256,768]{1,0:T(8,128)}, u32[]{:S(2)}, u32[]{:S(2)}) collective-permute-start(f32[256,768]{1,0:T(8,128)} %fusion.74), channel_id=1, source_target_pairs={{0,1},{1,0},{2,3},{3,2},{4,5},{5,4},{6,7},{7,6},{8,9},{9,8},{10,11... | collective-permute-start | bytes 2359304 | tf_op jit(solution)/shard_map/ppermute | solution.py:49
  132.9 2.7 collective-permute-start.5
  133.5 15.1 %copy-start.62 = (f32[768]{0:T(1024)}, f32[768]{0:T(1024)S(1)}, u32[]{:S(2)}) copy-start(f32[768]{0:T(1024)S(1)} %mul.335) | copy-start | bytes 9220
  133.6 15.1 %copy-start.95 = (f32[768]{0:T(1024)}, f32[768]{0:T(1024)S(1)}, u32[]{:S(2)}) copy-start(f32[768]{0:T(1024)S(1)} %add.345) | copy-start | bytes 9220
  133.6 15.1 %copy-start.104 = (f32[1152]{0:T(1024)S(1)}, f32[1152]{0:T(1024)}, u32[]{:S(2)}) copy-start(f32[1152]{0:T(1024)} %get-tuple-element.149) | copy-start | bytes 13828
  137.4 13.7 %copy-start.76 = (f32[256]{0:T(256)}, f32[256]{0:T(256)S(1)}, u32[]{:S(2)}) copy-start(f32[256]{0:T(256)S(1)} %broadcast_multiply_fusion.9) | copy-start | bytes 3076
  151.9 14.8 %collective-permute-start.6 = (bf16[2,128,768]{2,1,0:T(8,128)(2,1)}, bf16[2,128,768]{2,1,0:T(8,128)(2,1)}, u32[]{:S(2)}, u32[]{:S(2)}) collective-permute-start(bf16[2,128,768]{2,1,0:T(8,128)(2,1)} %bitcast.30), channel_id=1, source_target_pairs={{0,4},{2,6},{1,5},{3,7},{8,12},{10,14},{9,13},{11,15},{16,20},{18,... | collective-permute-start | bytes 1179656 | tf_op jit(solution)/shard_map/ppermute | solution.py:55
  157.6 16.4 %collective-permute-start.7 = (bf16[2,128,768]{2,1,0:T(8,128)(2,1)}, bf16[2,128,768]{2,1,0:T(8,128)(2,1)}, u32[]{:S(2)}, u32[]{:S(2)}) collective-permute-start(bf16[2,128,768]{2,1,0:T(8,128)(2,1)} %bitcast.30), channel_id=1, source_target_pairs={{0,2},{2,4},{4,6},{1,3},{3,5},{5,7},{8,10},{10,12},{12,14},{9,11},... | collective-permute-start | bytes 1179656 | tf_op jit(solution)/shard_map/ppermute | solution.py:55
  162.8 15.7 %copy-start.38 = (bf16[2,128,6,64]{1,0,3,2:T(2,128)(2,1)}, bf16[2,128,6,64]{1,0,3,2:T(2,128)(2,1)S(1)}, u32[]{:S(2)}) copy-start(bf16[2,128,6,64]{1,0,3,2:T(2,128)(2,1)S(1)} %reshape.416) | copy-start | bytes 589828
  189.9 8.8 %collective-permute-start.8 = (f32[256,768]{1,0:T(8,128)}, f32[256,768]{1,0:T(8,128)}, u32[]{:S(2)}, u32[]{:S(2)}) collective-permute-start(f32[256,768]{1,0:T(8,128)} %fusion.71), channel_id=1, source_target_pairs={{0,1},{1,0},{2,3},{3,2},{4,5},{5,4},{6,7},{7,6},{8,9},{9,8},{10,11... | collective-permute-start | bytes 2359304 | tf_op jit(solution)/shard_map/ppermute | solution.py:49
  200.6 14.2 %copy-start.78 = (f32[256]{0:T(256)}, f32[256]{0:T(256)S(1)}, u32[]{:S(2)}) copy-start(f32[256]{0:T(256)S(1)} %broadcast_multiply_fusion.8) | copy-start | bytes 3076
  200.9 13.9 %copy-start.99 = (f32[256]{0:T(256)}, f32[256]{0:T(256)S(1)}, u32[]{:S(2)}) copy-start(f32[256]{0:T(256)S(1)} %add_rsqrt_fusion) | copy-start | bytes 3076
  209.5 2.8 collective-permute-start.10
  212.0 2.8 collective-permute-start.9
  239.6 14.4 %collective-permute-start.11 = (bf16[2,128,768]{2,1,0:T(8,128)(2,1)}, bf16[2,128,768]{2,1,0:T(8,128)(2,1)}, u32[]{:S(2)}, u32[]{:S(2)}) collective-permute-start(bf16[2,128,768]{2,1,0:T(8,128)(2,1)} %get-tuple-element.106), channel_id=1, source_target_pairs={{2,0},{4,2},{6,4},{3,1},{5,3},{7,5},{10,8},{12,10},{14,12},{11,9},... | collective-permute-start | bytes 1179656 | tf_op jit(solution)/shard_map/ppermute | solution.py:60
  240.9 16.2 %collective-permute-start.12 = (bf16[2,128,768]{2,1,0:T(8,128)(2,1)}, bf16[2,128,768]{2,1,0:T(8,128)(2,1)}, u32[]{:S(2)}, u32[]{:S(2)}) collective-permute-start(bf16[2,128,768]{2,1,0:T(8,128)(2,1)} %get-tuple-element.107), channel_id=1, source_target_pairs={{4,0},{6,2},{5,1},{7,3},{12,8},{14,10},{13,9},{15,11},{20,16},{22,... | collective-permute-start | bytes 1179656 | tf_op jit(solution)/shard_map/ppermute | solution.py:60
  246.2 13.5 %copy-start.50 = (bf16[256,384]{1,0:T(8,128)(2,1)S(1)}, bf16[256,384]{1,0:T(8,128)(2,1)}, u32[]{:S(2)}) copy-start(bf16[256,384]{1,0:T(8,128)(2,1)} %copy.187) | copy-start | bytes 589828
  262.1 2.0 collective-permute-start.13
  270.0 2.1 collective-permute-start.14
  271.7 157.4 %reduce-scatter.5.cloned.1.call-start = ((), (), s32[]{:S(2)}) async-start(), calls=%async_computation.8 | async-start | bytes 2506752 | tf_op jit(solution)/shard_map/reduce_scatter | solution.py:212
  293.6 20.0 %collective-permute-start.15 = (bf16[2,128,768]{2,1,0:T(8,128)(2,1)}, bf16[2,128,768]{2,1,0:T(8,128)(2,1)}, u32[]{:S(2)}, u32[]{:S(2)}) collective-permute-start(bf16[2,128,768]{2,1,0:T(8,128)(2,1)} %get-tuple-element.104), channel_id=1, source_target_pairs={{2,0},{4,2},{6,4},{3,1},{5,3},{7,5},{10,8},{12,10},{14,12},{11,9},... | collective-permute-start | bytes 1179656 | tf_op jit(solution)/shard_map/ppermute | solution.py:60
  294.9 21.9 %collective-permute-start.16 = (bf16[2,128,768]{2,1,0:T(8,128)(2,1)}, bf16[2,128,768]{2,1,0:T(8,128)(2,1)}, u32[]{:S(2)}, u32[]{:S(2)}) collective-permute-start(bf16[2,128,768]{2,1,0:T(8,128)(2,1)} %get-tuple-element.105), channel_id=1, source_target_pairs={{4,0},{6,2},{5,1},{7,3},{12,8},{14,10},{13,9},{15,11},{20,16},{22,... | collective-permute-start | bytes 1179656 | tf_op jit(solution)/shard_map/ppermute | solution.py:60
  298.1 20.8 %copy-start.48 = (bf16[256,384]{1,0:T(8,128)(2,1)}, bf16[256,384]{1,0:T(8,128)(2,1)S(1)}, u32[]{:S(2)}) copy-start(bf16[256,384]{1,0:T(8,128)(2,1)S(1)} %copy.196) | copy-start | bytes 589828
  298.1 18.7 %copy-start.17 = (f32[2,384,384]{2,1,0:T(8,128)S(1)}, f32[2,384,384]{2,1,0:T(8,128)}, u32[]{:S(2)}) copy-start(f32[2,384,384]{2,1,0:T(8,128)} %copy-done.16) | copy-start | bytes 3538948
  298.5 20.4 %copy-start.43 = (bf16[256,768]{1,0:T(8,128)(2,1)S(1)}, bf16[256,768]{1,0:T(8,128)(2,1)}, u32[]{:S(2)}) copy-start(bf16[256,768]{1,0:T(8,128)(2,1)} %copy-done.42) | copy-start | bytes 1179652
  321.3 188.7 %reduce-scatter.11.cloned.1.call-start = ((), (), s32[]{:S(2)}) async-start(), calls=%async_computation.11 | async-start | bytes 5013504 | tf_op jit(solution)/shard_map/reduce_scatter | solution.py:212
  328.2 262.7 %reduce-scatter.9.cloned.1.call-start = ((), (), s32[]{:S(2)}) async-start(), calls=%async_computation.10 | async-start | bytes 5013504 | tf_op jit(solution)/shard_map/reduce_scatter | solution.py:212
  343.3 6.8 %collective-permute-start.17 = (bf16[256,768]{1,0:T(8,128)(2,1)S(1)}, bf16[256,768]{1,0:T(8,128)(2,1)S(1)}, u32[]{:S(2)}, u32[]{:S(2)}) collective-permute-start(bf16[256,768]{1,0:T(8,128)(2,1)S(1)} %fusion.36), channel_id=1, source_target_pairs={{0,1},{1,0},{2,3},{3,2},{4,5},{5,4},{6,7},{7,6},{8,9},{9,8},{10,11... | collective-permute-start | bytes 1179656 | tf_op jit(solution)/shard_map/ppermute | solution.py:49
  349.0 26.3 %copy-start.83 = (f32[256]{0:T(256)S(1)}, f32[256]{0:T(256)}, u32[]{:S(2)}) copy-start(f32[256]{0:T(256)} %copy-done.82) | copy-start | bytes 3076
  352.5 12.9 %all-to-all-start.1 = ((f32[16,8,128]{2,1,0:T(8,128)}), f32[16,8,128]{2,1,0:T(8,128)S(1)}, u32[]{:S(2)}, u32[]{:S(2)}) async-start(f32[16,8,128]{2,1,0:T(8,128)} %bitcast.123), calls=%async_computation.3 | async-start | bytes 131072 | tf_op jit(solution)/shard_map/all_to_all | solution.py:313
  365.5 11.0 %collective-permute-start.24 = (f32[8,128]{1,0:T(8,128)S(1)}, f32[8,128]{1,0:T(8,128)S(1)}, u32[]{:S(2)}, u32[]{:S(2)}) collective-permute-start(f32[8,128]{1,0:T(8,128)S(1)} %reduce_sum.395), channel_id=1, source_target_pairs={{0,2},{2,4},{4,6},{6,0},{1,3},{3,5},{5,7},{7,1},{8,10},{10,12},{12... | collective-permute-start | bytes 12296 | tf_op jit(solution)/shard_map/ppermute | solution.py:67
  372.5 5.1 collective-permute-start.25
  372.5 5.1 collective-permute-start.26
  377.7 7.7 %collective-permute-start.21 = (bf16[48,1536]{1,0:T(8,128)(2,1)}, bf16[48,1536]{1,0:T(8,128)(2,1)S(1)}, u32[]{:S(2)}, u32[]{:S(2)}) collective-permute-start(bf16[48,1536]{1,0:T(8,128)(2,1)} %reduce-scatter.7.cloned.1.call-done), channel_id=1, source_target_pairs={{0,2},{2,4},{4,6},{6,0},{1,3},{3,5},{5,7},{7,1},{8,10},{10,12},{12... | collective-permute-start | bytes 442376 | tf_op jit(solution)/shard_map/ppermute | solution.py:67
  377.8 8.8 %collective-permute-start.22 = (bf16[48,1536]{1,0:T(8,128)(2,1)}, bf16[48,1536]{1,0:T(8,128)(2,1)S(1)}, u32[]{:S(2)}, u32[]{:S(2)}) collective-permute-start(bf16[48,1536]{1,0:T(8,128)(2,1)} %reduce-scatter.7.cloned.1.call-done), channel_id=1, source_target_pairs={{0,4},{2,6},{4,0},{6,2},{1,5},{3,7},{5,1},{7,3},{8,12},{10,14},{12... | collective-permute-start | bytes 442376 | tf_op jit(solution)/shard_map/ppermute | solution.py:67
  381.7 5.4 collective-permute-start.23
  429.1 7.9 %collective-permute-start.18 = (bf16[48,1536]{1,0:T(8,128)(2,1)}, bf16[48,1536]{1,0:T(8,128)(2,1)S(1)}, u32[]{:S(2)}, u32[]{:S(2)}) collective-permute-start(bf16[48,1536]{1,0:T(8,128)(2,1)} %reduce-scatter.5.cloned.1.call-done), channel_id=1, source_target_pairs={{0,2},{2,4},{4,6},{6,0},{1,3},{3,5},{5,7},{7,1},{8,10},{10,12},{12... | collective-permute-start | bytes 442376 | tf_op jit(solution)/shard_map/ppermute | solution.py:67
  430.6 8.0 %collective-permute-start.19 = (bf16[48,1536]{1,0:T(8,128)(2,1)}, bf16[48,1536]{1,0:T(8,128)(2,1)S(1)}, u32[]{:S(2)}, u32[]{:S(2)}) collective-permute-start(bf16[48,1536]{1,0:T(8,128)(2,1)} %reduce-scatter.5.cloned.1.call-done), channel_id=1, source_target_pairs={{0,4},{2,6},{4,0},{6,2},{1,5},{3,7},{5,1},{7,3},{8,12},{10,14},{12... | collective-permute-start | bytes 442376 | tf_op jit(solution)/shard_map/ppermute | solution.py:67
  433.3 5.4 collective-permute-start.20
  509.9 15.9 %copy-start.55 = (bf16[48,3072]{1,0:T(8,128)(2,1)S(1)}, bf16[48,3072]{1,0:T(8,128)(2,1)}, u32[]{:S(2)}) copy-start(bf16[48,3072]{1,0:T(8,128)(2,1)} %reduce-scatter.11.cloned.1.call-done) | copy-start | bytes 884740
  509.9 10.4 %collective-permute-start.30 = (bf16[48,3072]{1,0:T(8,128)(2,1)}, bf16[48,3072]{1,0:T(8,128)(2,1)S(1)}, u32[]{:S(2)}, u32[]{:S(2)}) collective-permute-start(bf16[48,3072]{1,0:T(8,128)(2,1)} %reduce-scatter.11.cloned.1.call-done), channel_id=1, source_target_pairs={{0,2},{2,4},{4,6},{6,0},{1,3},{3,5},{5,7},{7,1},{8,10},{10,12},{12... | collective-permute-start | bytes 884744 | tf_op jit(solution)/shard_map/ppermute | solution.py:67
  511.4 14.4 %collective-permute-start.31 = (bf16[48,3072]{1,0:T(8,128)(2,1)}, bf16[48,3072]{1,0:T(8,128)(2,1)S(1)}, u32[]{:S(2)}, u32[]{:S(2)}) collective-permute-start(bf16[48,3072]{1,0:T(8,128)(2,1)} %reduce-scatter.11.cloned.1.call-done), channel_id=1, source_target_pairs={{0,4},{2,6},{4,0},{6,2},{1,5},{3,7},{5,1},{7,3},{8,12},{10,14},{12... | collective-permute-start | bytes 884744 | tf_op jit(solution)/shard_map/ppermute | solution.py:67
  514.1 11.7 %collective-permute-start.32 = (bf16[48,3072]{1,0:T(8,128)(2,1)}, bf16[48,3072]{1,0:T(8,128)(2,1)S(1)}, u32[]{:S(2)}, u32[]{:S(2)}) collective-permute-start(bf16[48,3072]{1,0:T(8,128)(2,1)} %reduce-scatter.11.cloned.1.call-done), channel_id=1, source_target_pairs={{0,6},{2,0},{4,2},{6,4},{1,7},{3,1},{5,3},{7,5},{8,14},{10,8},{12,... | collective-permute-start | bytes 884744 | tf_op jit(solution)/shard_map/ppermute | solution.py:67
  590.9 10.4 %collective-permute-start.27 = (bf16[48,3072]{1,0:T(8,128)(2,1)}, bf16[48,3072]{1,0:T(8,128)(2,1)S(1)}, u32[]{:S(2)}, u32[]{:S(2)}) collective-permute-start(bf16[48,3072]{1,0:T(8,128)(2,1)} %reduce-scatter.9.cloned.1.call-done), channel_id=1, source_target_pairs={{0,2},{2,4},{4,6},{6,0},{1,3},{3,5},{5,7},{7,1},{8,10},{10,12},{12... | collective-permute-start | bytes 884744 | tf_op jit(solution)/shard_map/ppermute | solution.py:67
  592.3 14.4 %collective-permute-start.28 = (bf16[48,3072]{1,0:T(8,128)(2,1)}, bf16[48,3072]{1,0:T(8,128)(2,1)S(1)}, u32[]{:S(2)}, u32[]{:S(2)}) collective-permute-start(bf16[48,3072]{1,0:T(8,128)(2,1)} %reduce-scatter.9.cloned.1.call-done), channel_id=1, source_target_pairs={{0,4},{2,6},{4,0},{6,2},{1,5},{3,7},{5,1},{7,3},{8,12},{10,14},{12... | collective-permute-start | bytes 884744 | tf_op jit(solution)/shard_map/ppermute | solution.py:67
  595.0 11.7 %collective-permute-start.29 = (bf16[48,3072]{1,0:T(8,128)(2,1)}, bf16[48,3072]{1,0:T(8,128)(2,1)S(1)}, u32[]{:S(2)}, u32[]{:S(2)}) collective-permute-start(bf16[48,3072]{1,0:T(8,128)(2,1)} %reduce-scatter.9.cloned.1.call-done), channel_id=1, source_target_pairs={{0,6},{2,0},{4,2},{6,4},{1,7},{3,1},{5,3},{7,5},{8,14},{10,8},{12,... | collective-permute-start | bytes 884744 | tf_op jit(solution)/shard_map/ppermute | solution.py:67
  (96 other events, 326.9 us)
Sparse Core Ops, SparseCore 0:
  13.5 67.7 all-gather.2
  83.9 64.6 all-gather.4
  271.8 79.7 reduce-scatter.6
  354.8 74.2 reduce-scatter.4
  432.3 77.6 reduce-scatter.10
  513.1 77.6 reduce-scatter.8
where the time goes:
time: 627 us; the launch traced here: 617 us
  waiting for transfers between devices  323 us (52%)
  local copies, waits for them, and re-layouts  82.9 us (13%)
  starting transfers between devices  76.2 us (12%)
  matrix products  68.4 us (11%)
  other arithmetic  50.4 us (8%)
  between operations  16.2 us (3%)
    reduce_scatter x4, waiting for transfers between devices, scatter(): return lax.psum_scatter(packed, 'shard', scatter_dimension=0, tiled=True)  176 us
    all_gather x2, waiting for transfers between devices, per_device(): gathered.append(lax.all_gather(packed, 'shard', axis=0, tiled=True))  49.1 us
    dot_general x24, matrix products, dot(): lax.dot_general(left, right, (((left_dim,), (right_dim,)), ((), ())), pre...  46.1 us
    ppermute x15, starting transfers between devices, context_sum(): lax.ppermute(part, 'context', [(i, (i + steps) % size) for i in range(siz...  31.3 us
    ppermute x4, waiting for transfers between devices, from_after(): lax.ppermute(block, 'context', [(i + steps, i) for i in range(size - step...  29.2 us
    ppermute x15, waiting for transfers between devices, context_sum(): lax.ppermute(part, 'context', [(i, (i + steps) % size) for i in range(siz...  25.6 us
    ppermute x6, waiting for transfers between devices, from_before(): lax.ppermute(block, 'context', [(i, i + steps) for i in range(size - step...  25 us
    ppermute x6, starting transfers between devices, from_before(): lax.ppermute(block, 'context', [(i, i + steps) for i in range(size - step...  24.3 us
  transfers between devices with their start and end apart: 41, of which 26 were waited for; matrix products, arithmetic and copies ran while one was open for 19% of the time, Pallas kernels for 0%

commit v1 on v0

--- a/solution.py
+++ b/solution.py
@@ -10,6 +10,11 @@
 MASKED = -1e30
 HALF = jnp.bfloat16
 FULL = jnp.float32
+
+
+def exchange_gather(x, axis, along):
+    stack = jnp.stack([x] * lax.axis_size(axis))
+    return jnp.concatenate(lax.all_to_all(stack, axis, 0, 0), axis=along)
 
 
 def gelu_value(preact):
@@ -114,7 +119,7 @@
             ],
             axis=1,
         )
-        gathered.append(lax.all_gather(packed, "shard", axis=0, tiled=True))
+        gathered.append(exchange_gather(packed, "shard", 0))
     small_parts = [norm_gains, offsets, head_bias, hidden_bias]
     small_sizes = [part.size for part in small_parts]
     small_total = sum(small_sizes)

time: 627 us -> 733 us (1.17)
  waiting for transfers between devices: 323 us -> 402 us
  starting transfers between devices: 76.2 us -> 86.9 us
  local copies, waits for them, and re-layouts: 82.9 us -> 91.9 us
    all_to_all x0 -> x2, waiting for transfers between devices: none -> 138 us  [exchange_gather(): return jnp.concatenate(lax.all_to_all(stack, axis, 0, 0), axis=along)]
    all_gather x2 -> x0, waiting for transfers between devices: 49.1 us -> none  [per_device(): gathered.append(lax.all_gather(packed, 'shard', axis=0, tiled=True))]
    all_to_all x0 -> x2, starting transfers between devices: none -> 10.4 us  [exchange_gather(): return jnp.concatenate(lax.all_to_all(stack, axis, 0, 0), axis=along)]
    unnamed x253 -> x233, local copies, waits for them, and re-layouts: 22.8 us -> 23.3 us
  transfers between devices with their start and end apart: 41 -> 41, of which waited for: 26 -> 26; matrix products, arithmetic and copies ran while one was open for 19% -> 18% of each run, Pallas kernels for 0% -> 0%
where the time goes in v1:
time: 733 us; the launch traced here: 722 us
  waiting for transfers between devices  402 us (55%)
  local copies, waits for them, and re-layouts  91.9 us (13%)
  starting transfers between devices  86.9 us (12%)
  matrix products  75.4 us (10%)
  other arithmetic  50.2 us (7%)
  between operations  15.7 us (2%)
    reduce_scatter x4, waiting for transfers between devices, scatter(): return lax.psum_scatter(packed, 'shard', scatter_dimension=0, tiled=True)  177 us
    all_to_all x2, waiting for transfers between devices, exchange_gather(): return jnp.concatenate(lax.all_to_all(stack, axis, 0, 0), axis=along)  138 us
    dot_general x24, matrix products, dot(): lax.dot_general(left, right, (((left_dim,), (right_dim,)), ((), ())), pre...  53.1 us
    ppermute x15, starting transfers between devices, context_sum(): lax.ppermute(part, 'context', [(i, (i + steps) % size) for i in range(siz...  31.2 us
    ppermute x4, waiting for transfers between devices, from_after(): lax.ppermute(block, 'context', [(i + steps, i) for i in range(size - step...  29.1 us
    ppermute x15, waiting for transfers between devices, context_sum(): lax.ppermute(part, 'context', [(i, (i + steps) % size) for i in range(siz...  25.5 us
    ppermute x6, starting transfers between devices, from_before(): lax.ppermute(block, 'context', [(i, i + steps) for i in range(size - step...  24.6 us
    unnamed x233, local copies, waits for them, and re-layouts  23.3 us
  transfers between devices with their start and end apart: 41, of which 26 were waited for; matrix products, arithmetic and copies ran while one was open for 18% of the time, Pallas kernels for 0%

profile of v1, /device:TPU:0, one launch (start us, length us, event | category | flops | bytes accessed | tf_op | source)
XLA Modules:
  0.0 721.6 jit_solution(13641795393796039970)
XLA Ops:
  11.2 8.0 %all-to-all-start = ((bf16[16,8,128]{2,1,0:T(8,128)(2,1)}), bf16[16,8,128]{2,1,0:T(8,128)(2,1)S(1)}, u32[]{:S(2)}, u32[]{:S(2)}) async-start(bf16[16,8,128]{2,1,0:T(8,128)(2,1)} %broadcast_in_dim.34), calls=%async_computation | async-start | bytes 65536 | tf_op jit(solution)/shard_map/all_to_all | solution.py:132
  24.4 2.4 all-to-all-done
  26.8 3.6 stack.174
  30.4 5.0 all-to-all-start.1
  35.5 5.1 collective-permute-start.2
  40.6 2.6 collective-permute-start.3
  46.5 92.8 %all-to-all-done.1 = bf16[16,48,4608]{2,1,0:T(8,128)(2,1)} async-done(((bf16[16,48,4608]{2,1,0:T(8,128)(2,1)}), bf16[16,48,4608]{2,1,0:T(8,128)(2,1)}, u32[]{:S(2)}, u32[]{:S(2)}) %all-to-all-start.1) | async-done | bytes 7077920 | tf_op jit(solution)/shard_map/all_to_all | solution.py:17
  139.3 3.5 stack.175
  142.8 5.4 all-to-all-start.2
  148.8 2.2 fusion.2
  151.0 5.1 collective-permute-start
  156.2 2.6 collective-permute-start.1
  159.2 6.5 collective-permute-done
  165.7 5.3 collective-permute-done.1
  177.7 2.4 fusion.74
  191.7 2.5 convolution_add_fusion.3
  194.2 4.2 fusion.15
  204.3 45.3 %all-to-all-done.2 = bf16[16,48,4608]{2,1,0:T(8,128)(2,1)} async-done(((bf16[16,48,4608]{2,1,0:T(8,128)(2,1)}), bf16[16,48,4608]{2,1,0:T(8,128)(2,1)}, u32[]{:S(2)}, u32[]{:S(2)}) %all-to-all-start.2) | async-done | bytes 7077920 | tf_op jit(solution)/shard_map/all_to_all | solution.py:17
  249.6 2.5 fusion.3
  252.9 5.9 collective-permute-start.6
  258.8 3.3 collective-permute-start.7
  263.9 3.9 collective-permute-done.6
  267.9 4.4 collective-permute-done.7
  282.8 2.6 fusion.49
  285.7 2.5 fusion.71
  299.2 2.6 convolution_add_fusion.2
  301.8 4.2 fusion.135
  306.0 3.5 fusion.45
  310.0 3.6 fusion.9
  314.0 2.5 multiply_reduce_fusion
  316.5 3.5 fusion.119
  325.2 3.5 fusion.80
  330.6 2.7 copy.186
  333.3 2.7 fusion.100
  335.9 2.7 copy.185
  348.0 7.9 %collective-permute-done.11 = bf16[2,128,768]{2,1,0:T(8,128)(2,1)} collective-permute-done((bf16[2,128,768]{2,1,0:T(8,128)(2,1)}, bf16[2,128,768]{2,1,0:T(8,128)(2,1)}, u32[]{:S(2)}, u32[]{:S(2)}) %collective-permute-start.11) | collective-permute-done | bytes 393248 | tf_op jit(solution)/shard_map/ppermute | solution.py:65
  355.9 3.1 collective-permute-done.12
  361.4 2.3 fusion.39
  368.1 3.6 fusion.136
  371.7 3.5 fusion.42
  377.6 2.5 multiply_reduce_fusion.2
  388.0 2.7 copy.195
  403.7 15.0 %collective-permute-done.15 = bf16[2,128,768]{2,1,0:T(8,128)(2,1)} collective-permute-done((bf16[2,128,768]{2,1,0:T(8,128)(2,1)}, bf16[2,128,768]{2,1,0:T(8,128)(2,1)}, u32[]{:S(2)}, u32[]{:S(2)}) %collective-permute-start.15) | collective-permute-done | bytes 393248 | tf_op jit(solution)/shard_map/ppermute | solution.py:65
  418.7 3.2 collective-permute-done.16
  430.6 2.8 pad_maximum_fusion.1
  434.5 2.2 convolution_convert_fusion.3
  437.6 2.7 pad_maximum_fusion
  446.2 2.3 fusion.36
  457.8 5.1 all-to-all-start.3
  462.9 7.6 %all-to-all-done.3 = f32[16,8,128]{2,1,0:T(8,128)S(1)} async-done(((f32[16,8,128]{2,1,0:T(8,128)}), f32[16,8,128]{2,1,0:T(8,128)S(1)}, u32[]{:S(2)}, u32[]{:S(2)}) %all-to-all-start.3) | async-done | bytes 65568 | tf_op jit(solution)/shard_map/all_to_all | solution.py:318
  470.6 7.1 collective-permute-start.24
  477.7 2.8 collective-permute-start.26
  483.0 3.8 collective-permute-start.22
  493.2 41.1 %reduce-scatter.5.cloned.1.call-done = bf16[48,1536]{1,0:T(8,128)(2,1)} async-done(((bf16[768,1536]{1,0:T(8,128)(2,1)}), bf16[48,1536]{1,0:T(8,128)(2,1)}) %reduce-scatter.5.cloned.1.call-update) | async-done | bytes 147472 | tf_op jit(solution)/shard_map/reduce_scatter | solution.py:217
  535.8 2.7 collective-permute-start.19
  540.0 2.2 collective-permute-done.18
  544.8 70.4 %reduce-scatter.11.cloned.1.call-done = bf16[48,3072]{1,0:T(8,128)(2,1)} async-done(((bf16[768,3072]{1,0:T(8,128)(2,1)}), bf16[48,3072]{1,0:T(8,128)(2,1)}) %reduce-scatter.11.cloned.1.call-update) | async-done | bytes 294928 | tf_op jit(solution)/shard_map/reduce_scatter | solution.py:217
  616.6 2.8 collective-permute-start.31
  622.3 3.3 collective-permute-done.30
  625.7 5.4 collective-permute-done.31
  631.2 65.0 %reduce-scatter.9.cloned.1.call-done = bf16[48,3072]{1,0:T(8,128)(2,1)} async-done(((bf16[768,3072]{1,0:T(8,128)(2,1)}), bf16[48,3072]{1,0:T(8,128)(2,1)}) %reduce-scatter.9.cloned.1.call-update) | async-done | bytes 294928 | tf_op jit(solution)/shard_map/reduce_scatter | solution.py:217
  697.6 2.8 collective-permute-start.28
  701.8 4.8 collective-permute-done.27
  706.6 5.4 collective-permute-done.28
  (476 shorter events, 158.9 us)
Async XLA Ops:
  11.2 15.6 %all-to-all-start = ((bf16[16,8,128]{2,1,0:T(8,128)(2,1)}), bf16[16,8,128]{2,1,0:T(8,128)(2,1)S(1)}, u32[]{:S(2)}, u32[]{:S(2)}) async-start(bf16[16,8,128]{2,1,0:T(8,128)(2,1)} %broadcast_in_dim.34), calls=%async_computation | async-start | bytes 65536 | tf_op jit(solution)/shard_map/all_to_all | solution.py:132
  30.4 12.8 %copy-start.2 = (f32[2,128,768]{2,1,0:T(8,128)S(1)}, f32[2,128,768]{2,1,0:T(8,128)}, u32[]{:S(2)}) copy-start(f32[2,128,768]{2,1,0:T(8,128)} %param.11) | copy-start | bytes 2359300
  30.4 108.8 %all-to-all-start.1 = ((bf16[16,48,4608]{2,1,0:T(8,128)(2,1)}), bf16[16,48,4608]{2,1,0:T(8,128)(2,1)}, u32[]{:S(2)}, u32[]{:S(2)}) async-start(bf16[16,48,4608]{2,1,0:T(8,128)(2,1)} %stack.174), calls=%async_computation.1 | async-start | bytes 14155776 | tf_op jit(solution)/shard_map/all_to_all | solution.py:17
  35.5 123.3 %collective-permute-start.2 = (s32[2,128]{1,0:T(2,128)S(1)}, s32[2,128]{1,0:T(2,128)S(1)}, u32[]{:S(2)}, u32[]{:S(2)}) collective-permute-start(s32[2,128]{1,0:T(2,128)S(1)} %copy-done.103), channel_id=1, source_target_pairs={{0,4},{2,6},{1,5},{3,7},{8,12},{10,14},{9,13},{11,15},{16,20},{18,... | collective-permute-start | bytes 3080 | tf_op jit(solution)/shard_map/ppermute | solution.py:60
  40.6 118.2 %collective-permute-start.3 = (s32[2,128]{1,0:T(2,128)S(1)}, s32[2,128]{1,0:T(2,128)S(1)}, u32[]{:S(2)}, u32[]{:S(2)}) collective-permute-start(s32[2,128]{1,0:T(2,128)S(1)} %copy-done.103), channel_id=1, source_target_pairs={{0,2},{2,4},{4,6},{1,3},{3,5},{5,7},{8,10},{10,12},{12,14},{9,11},... | collective-permute-start | bytes 3080 | tf_op jit(solution)/shard_map/ppermute | solution.py:60
  43.3 99.4 %copy-start.78 = (f32[256]{0:T(256)}, f32[256]{0:T(256)S(1)}, u32[]{:S(2)}) copy-start(f32[256]{0:T(256)S(1)} %get-tuple-element.151) | copy-start | bytes 3076
  43.6 99.2 %copy-start.80 = (f32[256]{0:T(256)}, f32[256]{0:T(256)S(1)}, u32[]{:S(2)}) copy-start(f32[256]{0:T(256)S(1)} %rsqrt_bitcast_fusion) | copy-start | bytes 3076
  45.6 97.2 %copy-start.56 = (f32[768]{0:T(1024)}, f32[768]{0:T(1024)S(1)}, u32[]{:S(2)}) copy-start(f32[768]{0:T(1024)S(1)} %mul.315) | copy-start | bytes 9220
  46.5 102.4 %copy-start.42 = (bf16[256,768]{1,0:T(8,128)(2,1)}, bf16[256,768]{1,0:T(8,128)(2,1)S(1)}, u32[]{:S(2)}) copy-start(bf16[256,768]{1,0:T(8,128)(2,1)S(1)} %add_convert_fusion.3) | copy-start | bytes 1179652
  142.8 106.8 %all-to-all-start.2 = ((bf16[16,48,4608]{2,1,0:T(8,128)(2,1)}), bf16[16,48,4608]{2,1,0:T(8,128)(2,1)}, u32[]{:S(2)}, u32[]{:S(2)}) async-start(bf16[16,48,4608]{2,1,0:T(8,128)(2,1)} %stack.175), calls=%async_computation.2 | async-start | bytes 14155776 | tf_op jit(solution)/shard_map/all_to_all | solution.py:17
  148.2 334.8 %reduce-scatter.7.cloned.1.call-start = ((), (), s32[]{:S(2)}) async-start(), calls=%async_computation.9 | async-start | bytes 2506752 | tf_op jit(solution)/shard_map/reduce_scatter | solution.py:217
  151.0 14.7 %collective-permute-start = (bf16[2,128,768]{2,1,0:T(8,128)(2,1)S(1)}, bf16[2,128,768]{2,1,0:T(8,128)(2,1)S(1)}, u32[]{:S(2)}, u32[]{:S(2)}) collective-permute-start(bf16[2,128,768]{2,1,0:T(8,128)(2,1)S(1)} %bitcast.249), channel_id=1, source_target_pairs={{0,4},{2,6},{1,5},{3,7},{8,12},{10,14},{9,13},{11,15},{16,20},{18,... | collective-permute-start | bytes 1179656 | tf_op jit(solution)/shard_map/ppermute | solution.py:60
  156.2 14.8 %collective-permute-start.1 = (bf16[2,128,768]{2,1,0:T(8,128)(2,1)S(1)}, bf16[2,128,768]{2,1,0:T(8,128)(2,1)S(1)}, u32[]{:S(2)}, u32[]{:S(2)}) collective-permute-start(bf16[2,128,768]{2,1,0:T(8,128)(2,1)S(1)} %bitcast.250), channel_id=1, source_target_pairs={{0,2},{2,4},{4,6},{1,3},{3,5},{5,7},{8,10},{10,12},{12,14},{9,11},... | collective-permute-start | bytes 1179656 | tf_op jit(solution)/shard_map/ppermute | solution.py:60
  159.0 14.3 %copy-start.44 = (pred[2,128,384]{2,1,0:T(8,128)(4,1)}, pred[2,128,384]{2,1,0:T(8,128)(4,1)S(1)}, u32[]{:S(2)}) copy-start(pred[2,128,384]{2,1,0:T(8,128)(4,1)S(1)} %and_and_fusion) | copy-start | bytes 294916
  177.7 12.5 %copy-start.34 = (bf16[2,128,6,64]{1,0,3,2:T(2,128)(2,1)}, bf16[2,128,6,64]{1,0,3,2:T(2,128)(2,1)S(1)}, u32[]{:S(2)}) copy-start(bf16[2,128,6,64]{1,0,3,2:T(2,128)(2,1)S(1)} %copy.170) | copy-start | bytes 589828
  180.1 8.5 %collective-permute-start.4 = (f32[256,768]{1,0:T(8,128)}, f32[256,768]{1,0:T(8,128)}, u32[]{:S(2)}, u32[]{:S(2)}) collective-permute-start(f32[256,768]{1,0:T(8,128)} %fusion.74), channel_id=1, source_target_pairs={{0,1},{1,0},{2,3},{3,2},{4,5},{5,4},{6,7},{7,6},{8,9},{9,8},{10,11... | collective-permute-start | bytes 2359304 | tf_op jit(solution)/shard_map/ppermute | solution.py:54
  198.4 2.9 collective-permute-start.5
  199.3 50.3 %copy-start.60 = (f32[768]{0:T(1024)}, f32[768]{0:T(1024)S(1)}, u32[]{:S(2)}) copy-start(f32[768]{0:T(1024)S(1)} %mul.335) | copy-start | bytes 9220
  199.3 50.3 %copy-start.93 = (f32[768]{0:T(1024)}, f32[768]{0:T(1024)S(1)}, u32[]{:S(2)}) copy-start(f32[768]{0:T(1024)S(1)} %add.345) | copy-start | bytes 9220
  199.3 50.3 %copy-start.102 = (f32[1152]{0:T(1024)S(1)}, f32[1152]{0:T(1024)}, u32[]{:S(2)}) copy-start(f32[1152]{0:T(1024)} %get-tuple-element.149) | copy-start | bytes 13828
  203.2 48.9 %copy-start.74 = (f32[256]{0:T(256)}, f32[256]{0:T(256)S(1)}, u32[]{:S(2)}) copy-start(f32[256]{0:T(256)S(1)} %broadcast_multiply_fusion.9) | copy-start | bytes 3076
  204.3 47.8 %copy-start.85 = (f32[256]{0:T(256)}, f32[256]{0:T(256)S(1)}, u32[]{:S(2)}) copy-start(f32[256]{0:T(256)S(1)} %add_rsqrt_fusion.1) | copy-start | bytes 3076
  252.9 15.0 %collective-permute-start.6 = (bf16[2,128,768]{2,1,0:T(8,128)(2,1)}, bf16[2,128,768]{2,1,0:T(8,128)(2,1)}, u32[]{:S(2)}, u32[]{:S(2)}) collective-permute-start(bf16[2,128,768]{2,1,0:T(8,128)(2,1)} %bitcast.32), channel_id=1, source_target_pairs={{0,4},{2,6},{1,5},{3,7},{8,12},{10,14},{9,13},{11,15},{16,20},{18,... | collective-permute-start | bytes 1179656 | tf_op jit(solution)/shard_map/ppermute | solution.py:60
  258.8 13.5 %collective-permute-start.7 = (bf16[2,128,768]{2,1,0:T(8,128)(2,1)}, bf16[2,128,768]{2,1,0:T(8,128)(2,1)}, u32[]{:S(2)}, u32[]{:S(2)}) collective-permute-start(bf16[2,128,768]{2,1,0:T(8,128)(2,1)} %bitcast.32), channel_id=1, source_target_pairs={{0,2},{2,4},{4,6},{1,3},{3,5},{5,7},{8,10},{10,12},{12,14},{9,11},... | collective-permute-start | bytes 1179656 | tf_op jit(solution)/shard_map/ppermute | solution.py:60
  263.9 12.9 %copy-start.38 = (bf16[2,128,6,64]{1,0,3,2:T(2,128)(2,1)}, bf16[2,128,6,64]{1,0,3,2:T(2,128)(2,1)S(1)}, u32[]{:S(2)}) copy-start(bf16[2,128,6,64]{1,0,3,2:T(2,128)(2,1)S(1)} %reshape.428) | copy-start | bytes 589828
  285.7 11.3 %copy-start.36 = (bf16[2,128,6,64]{1,0,3,2:T(2,128)(2,1)}, bf16[2,128,6,64]{1,0,3,2:T(2,128)(2,1)S(1)}, u32[]{:S(2)}) copy-start(bf16[2,128,6,64]{1,0,3,2:T(2,128)(2,1)S(1)} %copy.177) | copy-start | bytes 589828
  288.2 8.8 %collective-permute-start.8 = (f32[256,768]{1,0:T(8,128)}, f32[256,768]{1,0:T(8,128)}, u32[]{:S(2)}, u32[]{:S(2)}) collective-permute-start(f32[256,768]{1,0:T(8,128)} %fusion.71), channel_id=1, source_target_pairs={{0,1},{1,0},{2,3},{3,2},{4,5},{5,4},{6,7},{7,6},{8,9},{9,8},{10,11... | collective-permute-start | bytes 2359304 | tf_op jit(solution)/shard_map/ppermute | solution.py:54
  298.9 17.6 %copy-start.76 = (f32[256]{0:T(256)}, f32[256]{0:T(256)S(1)}, u32[]{:S(2)}) copy-start(f32[256]{0:T(256)S(1)} %broadcast_multiply_fusion.8) | copy-start | bytes 3076
  299.2 17.3 %copy-start.97 = (f32[256]{0:T(256)}, f32[256]{0:T(256)S(1)}, u32[]{:S(2)}) copy-start(f32[256]{0:T(256)S(1)} %add_rsqrt_fusion) | copy-start | bytes 3076
  309.5 4.4 collective-permute-start.10
  313.6 2.8 collective-permute-start.9
  341.4 14.5 %collective-permute-start.11 = (bf16[2,128,768]{2,1,0:T(8,128)(2,1)}, bf16[2,128,768]{2,1,0:T(8,128)(2,1)}, u32[]{:S(2)}, u32[]{:S(2)}) collective-permute-start(bf16[2,128,768]{2,1,0:T(8,128)(2,1)} %get-tuple-element.106), channel_id=1, source_target_pairs={{2,0},{4,2},{6,4},{3,1},{5,3},{7,5},{10,8},{12,10},{14,12},{11,9},... | collective-permute-start | bytes 1179656 | tf_op jit(solution)/shard_map/ppermute | solution.py:65
  342.7 16.2 %collective-permute-start.12 = (bf16[2,128,768]{2,1,0:T(8,128)(2,1)}, bf16[2,128,768]{2,1,0:T(8,128)(2,1)}, u32[]{:S(2)}, u32[]{:S(2)}) collective-permute-start(bf16[2,128,768]{2,1,0:T(8,128)(2,1)} %get-tuple-element.107), channel_id=1, source_target_pairs={{4,0},{6,2},{5,1},{7,3},{12,8},{14,10},{13,9},{15,11},{20,16},{22,... | collective-permute-start | bytes 1179656 | tf_op jit(solution)/shard_map/ppermute | solution.py:65
  348.0 13.4 %copy-start.50 = (bf16[256,384]{1,0:T(8,128)(2,1)S(1)}, bf16[256,384]{1,0:T(8,128)(2,1)}, u32[]{:S(2)}) copy-start(bf16[256,384]{1,0:T(8,128)(2,1)} %copy.187) | copy-start | bytes 589828
  363.7 2.0 collective-permute-start.13
  375.3 2.1 collective-permute-start.14
  376.9 157.4 %reduce-scatter.5.cloned.1.call-start = ((), (), s32[]{:S(2)}) async-start(), calls=%async_computation.8 | async-start | bytes 2506752 | tf_op jit(solution)/shard_map/reduce_scatter | solution.py:217
  398.7 19.9 %collective-permute-start.15 = (bf16[2,128,768]{2,1,0:T(8,128)(2,1)}, bf16[2,128,768]{2,1,0:T(8,128)(2,1)}, u32[]{:S(2)}, u32[]{:S(2)}) collective-permute-start(bf16[2,128,768]{2,1,0:T(8,128)(2,1)} %get-tuple-element.104), channel_id=1, source_target_pairs={{2,0},{4,2},{6,4},{3,1},{5,3},{7,5},{10,8},{12,10},{14,12},{11,9},... | collective-permute-start | bytes 1179656 | tf_op jit(solution)/shard_map/ppermute | solution.py:65
  400.0 21.9 %collective-permute-start.16 = (bf16[2,128,768]{2,1,0:T(8,128)(2,1)}, bf16[2,128,768]{2,1,0:T(8,128)(2,1)}, u32[]{:S(2)}, u32[]{:S(2)}) collective-permute-start(bf16[2,128,768]{2,1,0:T(8,128)(2,1)} %get-tuple-element.105), channel_id=1, source_target_pairs={{4,0},{6,2},{5,1},{7,3},{12,8},{14,10},{13,9},{15,11},{20,16},{22,... | collective-permute-start | bytes 1179656 | tf_op jit(solution)/shard_map/ppermute | solution.py:65
  403.2 20.8 %copy-start.48 = (bf16[256,384]{1,0:T(8,128)(2,1)}, bf16[256,384]{1,0:T(8,128)(2,1)S(1)}, u32[]{:S(2)}) copy-start(bf16[256,384]{1,0:T(8,128)(2,1)S(1)} %copy.196) | copy-start | bytes 589828
  403.2 18.6 %copy-start.17 = (f32[2,384,384]{2,1,0:T(8,128)S(1)}, f32[2,384,384]{2,1,0:T(8,128)}, u32[]{:S(2)}) copy-start(f32[2,384,384]{2,1,0:T(8,128)} %copy-done.16) | copy-start | bytes 3538948
  403.7 20.4 %copy-start.43 = (bf16[256,768]{1,0:T(8,128)(2,1)S(1)}, bf16[256,768]{1,0:T(8,128)(2,1)}, u32[]{:S(2)}) copy-start(bf16[256,768]{1,0:T(8,128)(2,1)} %copy-done.42) | copy-start | bytes 1179652
  426.4 188.9 %reduce-scatter.11.cloned.1.call-start = ((), (), s32[]{:S(2)}) async-start(), calls=%async_computation.11 | async-start | bytes 5013504 | tf_op jit(solution)/shard_map/reduce_scatter | solution.py:217
  433.4 262.9 %reduce-scatter.9.cloned.1.call-start = ((), (), s32[]{:S(2)}) async-start(), calls=%async_computation.10 | async-start | bytes 5013504 | tf_op jit(solution)/shard_map/reduce_scatter | solution.py:217
  446.2 9.1 %copy-start.79 = (f32[256]{0:T(256)S(1)}, f32[256]{0:T(256)}, u32[]{:S(2)}) copy-start(f32[256]{0:T(256)} %copy-done.78) | copy-start | bytes 3076
  448.5 6.8 collective-permute-start.17
  454.2 26.3 %copy-start.81 = (f32[256]{0:T(256)S(1)}, f32[256]{0:T(256)}, u32[]{:S(2)}) copy-start(f32[256]{0:T(256)} %copy-done.80) | copy-start | bytes 3076
  457.8 12.8 %all-to-all-start.3 = ((f32[16,8,128]{2,1,0:T(8,128)}), f32[16,8,128]{2,1,0:T(8,128)S(1)}, u32[]{:S(2)}, u32[]{:S(2)}) async-start(f32[16,8,128]{2,1,0:T(8,128)} %bitcast.125), calls=%async_computation.5 | async-start | bytes 131072 | tf_op jit(solution)/shard_map/all_to_all | solution.py:318
  470.6 11.0 %collective-permute-start.24 = (f32[8,128]{1,0:T(8,128)S(1)}, f32[8,128]{1,0:T(8,128)S(1)}, u32[]{:S(2)}, u32[]{:S(2)}) collective-permute-start(f32[8,128]{1,0:T(8,128)S(1)} %reduce_sum.395), channel_id=1, source_target_pairs={{0,2},{2,4},{4,6},{6,0},{1,3},{3,5},{5,7},{7,1},{8,10},{10,12},{12... | collective-permute-start | bytes 12296 | tf_op jit(solution)/shard_map/ppermute | solution.py:72
  477.7 5.1 collective-permute-start.25
  477.7 5.1 collective-permute-start.26
  482.9 7.7 %collective-permute-start.21 = (bf16[48,1536]{1,0:T(8,128)(2,1)}, bf16[48,1536]{1,0:T(8,128)(2,1)S(1)}, u32[]{:S(2)}, u32[]{:S(2)}) collective-permute-start(bf16[48,1536]{1,0:T(8,128)(2,1)} %reduce-scatter.7.cloned.1.call-done), channel_id=1, source_target_pairs={{0,2},{2,4},{4,6},{6,0},{1,3},{3,5},{5,7},{7,1},{8,10},{10,12},{12... | collective-permute-start | bytes 442376 | tf_op jit(solution)/shard_map/ppermute | solution.py:72
  483.0 8.8 %collective-permute-start.22 = (bf16[48,1536]{1,0:T(8,128)(2,1)}, bf16[48,1536]{1,0:T(8,128)(2,1)S(1)}, u32[]{:S(2)}, u32[]{:S(2)}) collective-permute-start(bf16[48,1536]{1,0:T(8,128)(2,1)} %reduce-scatter.7.cloned.1.call-done), channel_id=1, source_target_pairs={{0,4},{2,6},{4,0},{6,2},{1,5},{3,7},{5,1},{7,3},{8,12},{10,14},{12... | collective-permute-start | bytes 442376 | tf_op jit(solution)/shard_map/ppermute | solution.py:72
  486.9 5.4 collective-permute-start.23
  534.3 7.9 %collective-permute-start.18 = (bf16[48,1536]{1,0:T(8,128)(2,1)}, bf16[48,1536]{1,0:T(8,128)(2,1)S(1)}, u32[]{:S(2)}, u32[]{:S(2)}) collective-permute-start(bf16[48,1536]{1,0:T(8,128)(2,1)} %reduce-scatter.5.cloned.1.call-done), channel_id=1, source_target_pairs={{0,2},{2,4},{4,6},{6,0},{1,3},{3,5},{5,7},{7,1},{8,10},{10,12},{12... | collective-permute-start | bytes 442376 | tf_op jit(solution)/shard_map/ppermute | solution.py:72
  535.8 8.0 %collective-permute-start.19 = (bf16[48,1536]{1,0:T(8,128)(2,1)}, bf16[48,1536]{1,0:T(8,128)(2,1)S(1)}, u32[]{:S(2)}, u32[]{:S(2)}) collective-permute-start(bf16[48,1536]{1,0:T(8,128)(2,1)} %reduce-scatter.5.cloned.1.call-done), channel_id=1, source_target_pairs={{0,4},{2,6},{4,0},{6,2},{1,5},{3,7},{5,1},{7,3},{8,12},{10,14},{12... | collective-permute-start | bytes 442376 | tf_op jit(solution)/shard_map/ppermute | solution.py:72
  538.5 5.4 collective-permute-start.20
  615.3 15.8 %copy-start.53 = (bf16[48,3072]{1,0:T(8,128)(2,1)S(1)}, bf16[48,3072]{1,0:T(8,128)(2,1)}, u32[]{:S(2)}) copy-start(bf16[48,3072]{1,0:T(8,128)(2,1)} %reduce-scatter.11.cloned.1.call-done) | copy-start | bytes 884740
  615.3 10.4 %collective-permute-start.30 = (bf16[48,3072]{1,0:T(8,128)(2,1)}, bf16[48,3072]{1,0:T(8,128)(2,1)S(1)}, u32[]{:S(2)}, u32[]{:S(2)}) collective-permute-start(bf16[48,3072]{1,0:T(8,128)(2,1)} %reduce-scatter.11.cloned.1.call-done), channel_id=1, source_target_pairs={{0,2},{2,4},{4,6},{6,0},{1,3},{3,5},{5,7},{7,1},{8,10},{10,12},{12... | collective-permute-start | bytes 884744 | tf_op jit(solution)/shard_map/ppermute | solution.py:72
  616.6 14.4 %collective-permute-start.31 = (bf16[48,3072]{1,0:T(8,128)(2,1)}, bf16[48,3072]{1,0:T(8,128)(2,1)S(1)}, u32[]{:S(2)}, u32[]{:S(2)}) collective-permute-start(bf16[48,3072]{1,0:T(8,128)(2,1)} %reduce-scatter.11.cloned.1.call-done), channel_id=1, source_target_pairs={{0,4},{2,6},{4,0},{6,2},{1,5},{3,7},{5,1},{7,3},{8,12},{10,14},{12... | collective-permute-start | bytes 884744 | tf_op jit(solution)/shard_map/ppermute | solution.py:72
  619.5 11.6 %collective-permute-start.32 = (bf16[48,3072]{1,0:T(8,128)(2,1)}, bf16[48,3072]{1,0:T(8,128)(2,1)S(1)}, u32[]{:S(2)}, u32[]{:S(2)}) collective-permute-start(bf16[48,3072]{1,0:T(8,128)(2,1)} %reduce-scatter.11.cloned.1.call-done), channel_id=1, source_target_pairs={{0,6},{2,0},{4,2},{6,4},{1,7},{3,1},{5,3},{7,5},{8,14},{10,8},{12,... | collective-permute-start | bytes 884744 | tf_op jit(solution)/shard_map/ppermute | solution.py:72
  696.3 10.4 %collective-permute-start.27 = (bf16[48,3072]{1,0:T(8,128)(2,1)}, bf16[48,3072]{1,0:T(8,128)(2,1)S(1)}, u32[]{:S(2)}, u32[]{:S(2)}) collective-permute-start(bf16[48,3072]{1,0:T(8,128)(2,1)} %reduce-scatter.9.cloned.1.call-done), channel_id=1, source_target_pairs={{0,2},{2,4},{4,6},{6,0},{1,3},{3,5},{5,7},{7,1},{8,10},{10,12},{12... | collective-permute-start | bytes 884744 | tf_op jit(solution)/shard_map/ppermute | solution.py:72
  697.6 14.4 %collective-permute-start.28 = (bf16[48,3072]{1,0:T(8,128)(2,1)}, bf16[48,3072]{1,0:T(8,128)(2,1)S(1)}, u32[]{:S(2)}, u32[]{:S(2)}) collective-permute-start(bf16[48,3072]{1,0:T(8,128)(2,1)} %reduce-scatter.9.cloned.1.call-done), channel_id=1, source_target_pairs={{0,4},{2,6},{4,0},{6,2},{1,5},{3,7},{5,1},{7,3},{8,12},{10,14},{12... | collective-permute-start | bytes 884744 | tf_op jit(solution)/shard_map/ppermute | solution.py:72
  700.4 11.6 %collective-permute-start.29 = (bf16[48,3072]{1,0:T(8,128)(2,1)}, bf16[48,3072]{1,0:T(8,128)(2,1)S(1)}, u32[]{:S(2)}, u32[]{:S(2)}) collective-permute-start(bf16[48,3072]{1,0:T(8,128)(2,1)} %reduce-scatter.9.cloned.1.call-done), channel_id=1, source_target_pairs={{0,6},{2,0},{4,2},{6,4},{1,7},{3,1},{5,3},{7,5},{8,14},{10,8},{12,... | collective-permute-start | bytes 884744 | tf_op jit(solution)/shard_map/ppermute | solution.py:72
  (86 other events, 257.3 us)
Sparse Core Ops, SparseCore 0:
  377.0 79.6 reduce-scatter.6
  460.0 74.2 reduce-scatter.4
  537.6 77.6 reduce-scatter.10
  618.5 77.7 reduce-scatter.8
